TPU v7x, 128 devices: a whole 4x4x4 slice. The times are simulated.
128 devices in a mesh: leaf: 16 (over x, y), side: 8 (over z, core).
Axes of the slice: x: 4, y: 4, z: 4, core: 2. Of those that a mesh axis runs over, the one named last changes fastest.
Arguments:
- block: float32 [131072, 512], P(('leaf', 'side')), may hold values from -24 to 24
- basis: float32 [131072, 1024], P(('leaf', 'side')), may hold values from -1 to 1
Outputs:
- ortho: float32 [131072, 512], P(('leaf', 'side'))
- factor: float32 [512, 512], replicated
- coeffs: float32 [1024, 512], replicated
All inputs are finite; a program needn't handle non-finite values.
Results may differ from a plain program's by a relative error of at most 0.0001.
Values sent between devices are 32-bit elements; how exact they have to be, the bound alone decides.
A program may use at most 64 MiB of HBM per device.

v0:
```python
import jax
import jax.numpy as jnp
from jax import lax
from jax.sharding import PartitionSpec as P


def inner(left, right):
    return lax.dot_general(
        left,
        right,
        (((0,), (0,)), ((), ())),
        precision=lax.Precision.HIGHEST,
        preferred_element_type=jnp.float32,
    )


def product(left, right):
    return jnp.dot(left, right, precision=lax.Precision.HIGHEST, preferred_element_type=jnp.float32)


def small_upper(matrix):
    width = matrix.shape[0]
    positions = jnp.arange(width, dtype=jnp.int32)

    def one_step(column, carry):
        rest, result = carry
        column = jnp.asarray(column).astype(jnp.int32)
        row = lax.dynamic_slice_in_dim(rest, column, 1, 0)[0]
        pivot = jnp.sqrt(jnp.sum(jnp.where(positions == column, row, jnp.float32(0.0))))
        new_row = jnp.where(positions >= column, row / pivot, jnp.float32(0.0))
        result = lax.dynamic_update_slice_in_dim(result, new_row[None, :], column, 0)
        rest = rest - new_row[:, None] * new_row[None, :]
        return (rest, result)

    start = (matrix, jnp.zeros_like(matrix))
    return lax.fori_loop(0, width, one_step, start)[1]


def small_inverse(upper_block):
    width = upper_block.shape[0]
    positions = jnp.arange(width, dtype=jnp.int32)

    def one_step(count, result):
        index = (width - 1 - jnp.asarray(count)).astype(jnp.int32)
        row = lax.dynamic_slice_in_dim(upper_block, index, 1, 0)[0]
        pivot = jnp.sum(jnp.where(positions == index, row, jnp.float32(0.0)))
        beyond = jnp.where(positions > index, row, jnp.float32(0.0))
        unit = jnp.where(positions == index, jnp.float32(1.0), jnp.float32(0.0))
        new_row = (unit - product(beyond[None, :], result)[0]) / pivot
        return lax.dynamic_update_slice_in_dim(result, new_row[None, :], index, 0)

    return lax.fori_loop(0, width, one_step, jnp.zeros_like(upper_block))


def factor_and_inverse(gram):
    width = gram.shape[0]
    piece = min(128, width)
    count = width // piece
    rest = gram
    strips = []
    diag_inverses = []
    for index in range(count):
        diag = small_upper(rest[:piece, :piece])
        diag_inv = small_inverse(diag)
        right = product(diag_inv.T, rest[:piece, piece:])
        left_zeros = jnp.zeros((piece, index * piece), gram.dtype)
        strips.append(jnp.concatenate([left_zeros, diag, right], axis=1))
        diag_inverses.append(diag_inv)
        rest = rest[piece:, piece:] - inner(right, right)
    factor = jnp.concatenate(strips, axis=0)
    lower_part = None
    for index in reversed(range(count)):
        diag_inv = diag_inverses[index]
        if lower_part is None:
            lower_part = diag_inv
        else:
            coupling = factor[index * piece : (index + 1) * piece, (index + 1) * piece :]
            far = -product(diag_inv, product(coupling, lower_part))
            top = jnp.concatenate([diag_inv, far], axis=1)
            below = jnp.concatenate(
                [jnp.zeros((lower_part.shape[0], piece), gram.dtype), lower_part], axis=1
            )
            lower_part = jnp.concatenate([top, below], axis=0)
    return (factor, lower_part)


def shards(block, basis):
    rows_total = block.shape[0] * lax.axis_size("leaf") * lax.axis_size("side")
    coeffs = lax.psum(inner(basis, block), ("leaf", "side"))
    projected = block - product(basis, coeffs)
    local_gram = inner(projected, projected) / rows_total
    factor, inverse = factor_and_inverse(lax.psum(local_gram, ("leaf", "side")))
    ortho = product(projected, inverse)
    return (ortho, factor, coeffs)


def solution(mesh):
    return jax.shard_map(
        shards,
        mesh=mesh,
        in_specs=(P(("leaf", "side"), None), P(("leaf", "side"), None)),
        out_specs=(P(("leaf", "side"), None), P(), P()),
        check_vma=False,
    )
```

profile of v0, /device:TPU:1, one launch (start us, length us, event | category | flops | bytes accessed | tf_op | source)
XLA Modules:
  0.0 1886.3 jit_solution(14410040137876746820)
XLA Ops:
  7.2 10.2 fusion.74
  17.7 1.3 copy-done
  19.0 1.8 copy.5
  20.8 150.3 %all-reduce.7.cloned.1.call-done = f32[1024,512]{1,0:T(8,128)} async-done(((f32[1024,512]{1,0:T(8,128)}), f32[1024,512]{1,0:T(8,128)}) %all-reduce.7.cloned.1.call-update) | async-done | bytes 2097168 | tf_op jit(solution)/shard_map/psum | solution.py:89
  171.2 16.2 bitcast_subtract_fusion
  187.3 4.5 convolution_multiply_fusion
  191.8 145.8 %all-reduce.9.cloned.1.call-done = f32[512,512]{1,0:T(8,128)} async-done(((f32[512,512]{1,0:T(8,128)}), f32[512,512]{1,0:T(8,128)}) %all-reduce.9.cloned.1.call-update) | async-done | bytes 1048592 | tf_op jit(solution)/shard_map/psum | solution.py:92
  337.6 0.8 slice.36
  338.5 192.5 %while.136 = (s32[]{:T(128)}, f32[128,128]{1,0:T(8,128)S(1)}, f32[128,128]{1,0:T(8,128)S(1)}, s32[]{:T(128)}, s32[]{:T(128)}) while((s32[]{:T(128)}, f32[128,128]{1,0:T(8,128)S(1)}, f32[128,128]{1,0:T(8,128)S(1)}, s32[]{:T(128)}, s32[]{:T(128)}) %tuple.273), condition=%wide.region_4.5_spmd.clone.clone, body=%wide.region_2.4_spmd.clone.clone.sunk | while | flops 34305 | bytes 142421 | solution.py:36
  531.0 187.3 %while.137 = (s32[]{:T(128)}, f32[128,128]{1,0:T(8,128)S(1)}, f32[128,128]{1,0:T(8,128)S(1)}, s32[]{:T(128)}, s32[]{:T(128)}, /*index=5*/s32[]{:T(128)}, s32[]{:T(128)}) while((s32[]{:T(128)}, f32[128,128]{1,0:T(8,128)S(1)}, f32[128,128]{1,0:T(8,128)S(1)}, s32[]{:T(128)}, s32[]{:T(128)}, /*index=5*/s32[]{:T(128)}, ...), condition=%wide.region_7.8_spmd.clone.clone, body=%wide.region_5.7_spmd.clone.clone.sunk | while | flops 197765 | bytes 69783 | solution.py:52
  531.6 0.8 fusion.139
  557.9 0.8 fusion.139
  559.4 0.8 fusion.139
  585.7 0.8 fusion.139
  587.1 0.8 fusion.139
  613.4 0.8 fusion.139
  614.9 0.8 fusion.139
  641.2 0.8 fusion.139
  642.7 0.8 fusion.139
  669.0 0.8 fusion.139
  670.4 0.8 fusion.139
  696.8 0.8 fusion.139
  698.2 0.8 fusion.139
  718.9 1.3 fusion.63
  720.2 1.7 convolution_subtract_fusion
  722.0 192.5 %while.138 = (s32[]{:T(128)}, f32[128,128]{1,0:T(8,128)S(1)}, f32[128,128]{1,0:T(8,128)S(1)}, s32[]{:T(128)}, s32[]{:T(128)}) while((s32[]{:T(128)}, f32[128,128]{1,0:T(8,128)S(1)}, f32[128,128]{1,0:T(8,128)S(1)}, s32[]{:T(128)}, s32[]{:T(128)}) %tuple.279), condition=%wide.region_10.11_spmd.clone.clone, body=%wide.region_8.10_spmd.clone.clone.sunk | while | flops 34305 | bytes 142421 | solution.py:36
  914.5 187.1 %while.139 = (s32[]{:T(128)}, f32[128,128]{1,0:T(8,128)S(1)}, f32[128,128]{1,0:T(8,128)S(1)}, s32[]{:T(128)}, s32[]{:T(128)}, /*index=5*/s32[]{:T(128)}, s32[]{:T(128)}) while((s32[]{:T(128)}, f32[128,128]{1,0:T(8,128)S(1)}, f32[128,128]{1,0:T(8,128)S(1)}, s32[]{:T(128)}, s32[]{:T(128)}, /*index=5*/s32[]{:T(128)}, ...), condition=%wide.region_13.14_spmd.clone.clone, body=%wide.region_11.13_spmd.clone.clone.sunk | while | flops 197765 | bytes 69783 | solution.py:52
  918.0 0.8 fusion.145
  919.5 0.8 fusion.145
  945.8 0.8 fusion.145
  947.2 0.8 fusion.145
  973.5 0.8 fusion.145
  975.0 0.8 fusion.145
  1001.3 0.8 fusion.145
  1002.8 0.8 fusion.145
  1029.1 0.8 fusion.145
  1030.5 0.8 fusion.145
  1056.9 0.8 fusion.145
  1102.9 192.5 %while.140 = (s32[]{:T(128)}, f32[128,128]{1,0:T(8,128)S(1)}, f32[128,128]{1,0:T(8,128)S(1)}, s32[]{:T(128)}, s32[]{:T(128)}) while((s32[]{:T(128)}, f32[128,128]{1,0:T(8,128)S(1)}, f32[128,128]{1,0:T(8,128)S(1)}, s32[]{:T(128)}, s32[]{:T(128)}) %tuple.285), condition=%wide.region_16.17_spmd.clone.clone, body=%wide.region_14.16_spmd.clone.clone.sunk | while | flops 34305 | bytes 142421 | solution.py:36
  1295.4 187.1 %while.141 = (s32[]{:T(128)}, f32[128,128]{1,0:T(8,128)S(1)}, f32[128,128]{1,0:T(8,128)S(1)}, s32[]{:T(128)}, s32[]{:T(128)}, /*index=5*/s32[]{:T(128)}, s32[]{:T(128)}) while((s32[]{:T(128)}, f32[128,128]{1,0:T(8,128)S(1)}, f32[128,128]{1,0:T(8,128)S(1)}, s32[]{:T(128)}, s32[]{:T(128)}, /*index=5*/s32[]{:T(128)}, ...), condition=%wide.region_19.20_spmd.clone.clone, body=%wide.region_17.19_spmd.clone.clone.sunk | while | flops 197765 | bytes 69783 | solution.py:52
  1483.7 192.5 %while.142 = (s32[]{:T(128)}, f32[128,128]{1,0:T(8,128)S(1)}, f32[128,128]{1,0:T(8,128)S(1)}, s32[]{:T(128)}, s32[]{:T(128)}) while((s32[]{:T(128)}, f32[128,128]{1,0:T(8,128)S(1)}, f32[128,128]{1,0:T(8,128)S(1)}, s32[]{:T(128)}, s32[]{:T(128)}) %tuple.291), condition=%wide.region_22.23_spmd.clone.clone, body=%wide.region_20.22_spmd.clone.clone.sunk | while | flops 34305 | bytes 142421 | solution.py:36
  1676.3 187.1 %while.143 = (s32[]{:T(128)}, f32[128,128]{1,0:T(8,128)S(1)}, f32[128,128]{1,0:T(8,128)S(1)}, s32[]{:T(128)}, s32[]{:T(128)}, /*index=5*/s32[]{:T(128)}, s32[]{:T(128)}) while((s32[]{:T(128)}, f32[128,128]{1,0:T(8,128)S(1)}, f32[128,128]{1,0:T(8,128)S(1)}, s32[]{:T(128)}, s32[]{:T(128)}, /*index=5*/s32[]{:T(128)}, ...), condition=%wide.region_25.26_spmd.clone.clone, body=%wide.region_23.25_spmd.clone.clone.sunk | while | flops 197765 | bytes 69783 | solution.py:52
  1865.1 1.4 fusion.73
  1866.7 1.4 convolution_negate_fusion
  1868.2 8.0 fusion.56
  1876.2 1.1 select_maximum_fusion
  1877.3 0.8 copy-done.1
  1878.1 1.3 copy.83
  (4633 shorter events, 1113.5 us)
Async XLA Ops:
  7.2 164.0 %all-reduce.7.cloned.1.call-start = ((), (), s32[]{:S(2)}) async-start(), calls=%async_computation | async-start | bytes 4194304 | tf_op jit(solution)/shard_map/psum | solution.py:89
  17.4 1.6 copy-start
  17.4 320.2 %all-reduce.9.cloned.1.call-start = ((), (), s32[]{:S(2)}) async-start(), calls=%async_computation.1 | async-start | bytes 2097152 | tf_op jit(solution)/shard_map/psum | solution.py:92
  718.3 0.6 copy-start.2
  1101.5 0.6 copy-start.4
  1482.5 0.6 copy-start.6
  1863.3 1.3 copy-start.8
  1868.1 8.1 copy-start.3
  1868.1 8.1 copy-start.5
  1868.2 8.1 copy-start.7
  1868.2 8.1 copy-start.9
  1876.2 2.0 copy-start.1
Sparse Core Ops, SparseCore 0:
  17.6 153.5 all-reduce.6
  192.0 145.6 all-reduce.8
where the time goes:
time: 1900 us; the launch traced here: 1890 us
  other arithmetic  685 us (36%)
  matrix products  455 us (24%)
  loops' own time  391 us (21%)
  waiting for transfers between devices  296 us (16%)
  local copies, waits for them, and re-layouts  43.5 us (2%)
    dot_general x523, matrix products, product(): jnp.dot(left, right, precision=lax.Precision.HIGHEST, preferred_element_t...  438 us
    another operation x4, loops' own time, small_upper(): return lax.fori_loop(0, width, one_step, start)[1]  377 us
    reduce_sum x512, other arithmetic, one_step(): pivot = jnp.sum(jnp.where(positions == index, row, jnp.float32(0.0)))  311 us
    reduce_sum x512, other arithmetic, one_step(): jnp.sum(jnp.where(positions == column, row, jnp.float32(0.0)))  310 us
    psum x1, waiting for transfers between devices, shards(): coeffs = lax.psum(inner(basis, block), ('leaf', 'side'))  150 us
    psum x1, waiting for transfers between devices, shards(): factor, inverse = factor_and_inverse(lax.psum(local_gram, ('leaf', 'side')))  146 us
    sub x512, other arithmetic, one_step(): rest = rest - new_row[:, None] * new_row[None, :]  42.1 us

commit v1 on v0

--- a/solution.py
+++ b/solution.py
@@ -2,6 +2,11 @@
 import jax.numpy as jnp
 from jax import lax
 from jax.sharding import PartitionSpec as P
+
+
+def by_each_axis(x, inner_axis, outer_axis):
+    half = lax.psum(x, inner_axis)
+    return lax.psum(half, outer_axis)
 
 
 def inner(left, right):
@@ -86,7 +91,7 @@
 
 def shards(block, basis):
     rows_total = block.shape[0] * lax.axis_size("leaf") * lax.axis_size("side")
-    coeffs = lax.psum(inner(basis, block), ("leaf", "side"))
+    coeffs = by_each_axis(inner(basis, block), "side", "leaf")
     projected = block - product(basis, coeffs)
     local_gram = inner(projected, projected) / rows_total
     factor, inverse = factor_and_inverse(lax.psum(local_gram, ("leaf", "side")))

time: 1900 us -> 1910 us (level)
    psum x1 -> x2, waiting for transfers between devices: 150 us -> 159 us  [the longest x1 91.6 us: by_each_axis(): return lax.psum(half, outer_axis)]
where the time goes in v1:
time: 1910 us; the launch traced here: 1900 us
  other arithmetic  685 us (36%)
  matrix products  455 us (24%)
  loops' own time  391 us (20%)
  waiting for transfers between devices  307 us (16%)
  local copies, waits for them, and re-layouts  42.2 us (2%)
    dot_general x523, matrix products, product(): jnp.dot(left, right, precision=lax.Precision.HIGHEST, preferred_element_t...  438 us
    another operation x4, loops' own time, small_upper(): return lax.fori_loop(0, width, one_step, start)[1]  377 us
    reduce_sum x512, other arithmetic, one_step(): pivot = jnp.sum(jnp.where(positions == index, row, jnp.float32(0.0)))  311 us
    reduce_sum x512, other arithmetic, one_step(): jnp.sum(jnp.where(positions == column, row, jnp.float32(0.0)))  310 us
    psum x1, waiting for transfers between devices, shards(): factor, inverse = factor_and_inverse(lax.psum(local_gram, ('leaf', 'side')))  148 us
    psum x1, waiting for transfers between devices, by_each_axis(): return lax.psum(half, outer_axis)  91.6 us
    psum x1, waiting for transfers between devices, by_each_axis(): half = lax.psum(x, inner_axis)  67.3 us
    sub x512, other arithmetic, one_step(): rest = rest - new_row[:, None] * new_row[None, :]  42.1 us

profile of v1, /device:TPU:1, one launch (start us, length us, event | category | flops | bytes accessed | tf_op | source)
XLA Modules:
  0.0 1895.5 jit_solution(2541943813805869805)
XLA Ops:
  7.2 10.2 fusion.74
  17.5 67.3 %all-reduce.8.cloned.1.call-done = f32[1024,512]{1,0:T(8,128)} async-done(((f32[1024,512]{1,0:T(8,128)}), f32[1024,512]{1,0:T(8,128)}) %all-reduce.8.cloned.1.call-update) | async-done | bytes 2097168 | tf_op jit(solution)/shard_map/psum | solution.py:8
  85.1 1.8 copy.5
  86.9 91.6 %all-reduce.10.cloned.1.call-done = f32[1024,512]{1,0:T(8,128)} async-done(((f32[1024,512]{1,0:T(8,128)}), f32[1024,512]{1,0:T(8,128)}) %all-reduce.10.cloned.1.call-update) | async-done | bytes 2097168 | tf_op jit(solution)/shard_map/psum | solution.py:9
  178.5 16.2 bitcast_subtract_fusion
  194.6 4.5 convolution_multiply_fusion
  199.1 148.0 %all-reduce.12.cloned.1.call-done = f32[512,512]{1,0:T(8,128)} async-done(((f32[512,512]{1,0:T(8,128)}), f32[512,512]{1,0:T(8,128)}) %all-reduce.12.cloned.1.call-update) | async-done | bytes 1048592 | tf_op jit(solution)/shard_map/psum | solution.py:97
  347.2 0.8 slice.36
  348.0 192.5 %while.136 = (s32[]{:T(128)}, f32[128,128]{1,0:T(8,128)S(1)}, f32[128,128]{1,0:T(8,128)S(1)}, s32[]{:T(128)}, s32[]{:T(128)}) while((s32[]{:T(128)}, f32[128,128]{1,0:T(8,128)S(1)}, f32[128,128]{1,0:T(8,128)S(1)}, s32[]{:T(128)}, s32[]{:T(128)}) %tuple.273), condition=%wide.region_5.6_spmd.clone.clone, body=%wide.region_3.5_spmd.clone.clone.sunk | while | flops 34305 | bytes 142421 | solution.py:41
  540.5 187.3 %while.137 = (s32[]{:T(128)}, f32[128,128]{1,0:T(8,128)S(1)}, f32[128,128]{1,0:T(8,128)S(1)}, s32[]{:T(128)}, s32[]{:T(128)}, /*index=5*/s32[]{:T(128)}, s32[]{:T(128)}) while((s32[]{:T(128)}, f32[128,128]{1,0:T(8,128)S(1)}, f32[128,128]{1,0:T(8,128)S(1)}, s32[]{:T(128)}, s32[]{:T(128)}, /*index=5*/s32[]{:T(128)}, ...), condition=%wide.region_8.9_spmd.clone.clone, body=%wide.region_6.8_spmd.clone.clone.sunk | while | flops 197765 | bytes 69783 | solution.py:57
  552.8 0.8 fusion.139
  554.3 0.8 fusion.139
  580.6 0.8 fusion.139
  582.1 0.8 fusion.139
  608.4 0.8 fusion.139
  609.8 0.8 fusion.139
  636.1 0.8 fusion.139
  637.6 0.8 fusion.139
  663.9 0.8 fusion.139
  665.4 0.8 fusion.139
  691.7 0.8 fusion.139
  693.1 0.8 fusion.139
  719.5 0.8 fusion.139
  720.9 0.8 fusion.139
  728.4 1.3 fusion.63
  729.7 1.7 convolution_subtract_fusion
  731.5 192.5 %while.138 = (s32[]{:T(128)}, f32[128,128]{1,0:T(8,128)S(1)}, f32[128,128]{1,0:T(8,128)S(1)}, s32[]{:T(128)}, s32[]{:T(128)}) while((s32[]{:T(128)}, f32[128,128]{1,0:T(8,128)S(1)}, f32[128,128]{1,0:T(8,128)S(1)}, s32[]{:T(128)}, s32[]{:T(128)}) %tuple.279), condition=%wide.region_11.12_spmd.clone.clone, body=%wide.region_9.11_spmd.clone.clone.sunk | while | flops 34305 | bytes 142421 | solution.py:41
  924.0 187.1 %while.139 = (s32[]{:T(128)}, f32[128,128]{1,0:T(8,128)S(1)}, f32[128,128]{1,0:T(8,128)S(1)}, s32[]{:T(128)}, s32[]{:T(128)}, /*index=5*/s32[]{:T(128)}, s32[]{:T(128)}) while((s32[]{:T(128)}, f32[128,128]{1,0:T(8,128)S(1)}, f32[128,128]{1,0:T(8,128)S(1)}, s32[]{:T(128)}, s32[]{:T(128)}, /*index=5*/s32[]{:T(128)}, ...), condition=%wide.region_14.15_spmd.clone.clone, body=%wide.region_12.14_spmd.clone.clone.sunk | while | flops 197765 | bytes 69783 | solution.py:57
  939.2 0.8 fusion.145
  940.7 0.8 fusion.145
  967.0 0.8 fusion.145
  968.5 0.8 fusion.145
  994.8 0.8 fusion.145
  996.2 0.8 fusion.145
  1022.6 0.8 fusion.145
  1024.0 0.8 fusion.145
  1050.3 0.8 fusion.145
  1051.8 0.8 fusion.145
  1112.5 192.5 %while.140 = (s32[]{:T(128)}, f32[128,128]{1,0:T(8,128)S(1)}, f32[128,128]{1,0:T(8,128)S(1)}, s32[]{:T(128)}, s32[]{:T(128)}) while((s32[]{:T(128)}, f32[128,128]{1,0:T(8,128)S(1)}, f32[128,128]{1,0:T(8,128)S(1)}, s32[]{:T(128)}, s32[]{:T(128)}) %tuple.285), condition=%wide.region_17.18_spmd.clone.clone, body=%wide.region_15.17_spmd.clone.clone.sunk | while | flops 34305 | bytes 142421 | solution.py:41
  1305.0 187.1 %while.141 = (s32[]{:T(128)}, f32[128,128]{1,0:T(8,128)S(1)}, f32[128,128]{1,0:T(8,128)S(1)}, s32[]{:T(128)}, s32[]{:T(128)}, /*index=5*/s32[]{:T(128)}, s32[]{:T(128)}) while((s32[]{:T(128)}, f32[128,128]{1,0:T(8,128)S(1)}, f32[128,128]{1,0:T(8,128)S(1)}, s32[]{:T(128)}, s32[]{:T(128)}, /*index=5*/s32[]{:T(128)}, ...), condition=%wide.region_20.21_spmd.clone.clone, body=%wide.region_18.20_spmd.clone.clone.sunk | while | flops 197765 | bytes 69783 | solution.py:57
  1493.2 192.5 %while.142 = (s32[]{:T(128)}, f32[128,128]{1,0:T(8,128)S(1)}, f32[128,128]{1,0:T(8,128)S(1)}, s32[]{:T(128)}, s32[]{:T(128)}) while((s32[]{:T(128)}, f32[128,128]{1,0:T(8,128)S(1)}, f32[128,128]{1,0:T(8,128)S(1)}, s32[]{:T(128)}, s32[]{:T(128)}) %tuple.291), condition=%wide.region_23.24_spmd.clone.clone, body=%wide.region_21.23_spmd.clone.clone.sunk | while | flops 34305 | bytes 142421 | solution.py:41
  1685.8 187.1 %while.143 = (s32[]{:T(128)}, f32[128,128]{1,0:T(8,128)S(1)}, f32[128,128]{1,0:T(8,128)S(1)}, s32[]{:T(128)}, s32[]{:T(128)}, /*index=5*/s32[]{:T(128)}, s32[]{:T(128)}) while((s32[]{:T(128)}, f32[128,128]{1,0:T(8,128)S(1)}, f32[128,128]{1,0:T(8,128)S(1)}, s32[]{:T(128)}, s32[]{:T(128)}, /*index=5*/s32[]{:T(128)}, ...), condition=%wide.region_26.27_spmd.clone.clone, body=%wide.region_24.26_spmd.clone.clone.sunk | while | flops 197765 | bytes 69783 | solution.py:57
  1874.7 1.4 fusion.73
  1876.3 1.4 convolution_negate_fusion
  1877.7 8.0 fusion.56
  1885.8 1.1 select_maximum_fusion
  1886.9 0.8 copy-done.1
  1887.7 1.3 copy.84
  (4636 shorter events, 1113.6 us)
Async XLA Ops:
  7.2 77.7 %all-reduce.8.cloned.1.call-start = ((), (), s32[]{:S(2)}) async-start(), calls=%async_computation | async-start | bytes 4194304 | tf_op jit(solution)/shard_map/psum | solution.py:8
  17.4 67.7 %copy-start = (f32[1024,512]{1,0:T(8,128)S(1)}, f32[1024,512]{1,0:T(8,128)}, u32[]{:S(2)}) copy-start(f32[1024,512]{1,0:T(8,128)} %param.18) | copy-start | bytes 6291460
  17.4 161.0 %all-reduce.10.cloned.1.call-start = ((), (), s32[]{:S(2)}) async-start(), calls=%async_computation.1 | async-start | bytes 4194304 | tf_op jit(solution)/shard_map/psum | solution.py:9
  84.8 262.3 %all-reduce.12.cloned.1.call-start = ((), (), s32[]{:S(2)}) async-start(), calls=%async_computation.2 | async-start | bytes 2097152 | tf_op jit(solution)/shard_map/psum | solution.py:97
  727.8 0.6 copy-start.2
  1111.1 0.6 copy-start.4
  1492.0 0.6 copy-start.6
  1872.9 1.3 copy-start.8
  1877.7 8.1 copy-start.3
  1877.7 8.1 copy-start.5
  1877.7 8.1 copy-start.7
  1877.7 8.1 copy-start.9
  1885.7 2.0 copy-start.1
Sparse Core Ops, SparseCore 0:
  17.6 67.2 all-reduce.7
  88.1 90.2 all-reduce.9
  199.3 147.8 all-reduce.11
